TPU v7x, 512 devices: a whole 4x4x16 slice. The times are simulated.
512 devices in a mesh: req: 64 (over z, x), head: 8 (over y, core).
Axes of the slice: x: 4, y: 4, z: 16, core: 2. Of those that a mesh axis runs over, the one named last changes fastest.
Arguments:
- tokens: bfloat16 [64, 512, 1024], P('req', 'head'), may hold values from -6 to 6
- gain: bfloat16 [1024], replicated, may hold values from 0.099609375 to 1.8984375
- projection_weight: bfloat16 [1024, 4, 1024], P(None, None, 'head'), may hold values from -0.1875 to 0.1875
- output_weight: bfloat16 [1024, 1024], P('head'), may hold values from -0.1875 to 0.1875
- persist: bfloat16 [2, 16, 1024], P(None, None, 'head'), may hold values from -6 to 6
- cache_page_slots: bfloat16 [64, 64, 64, 2, 1024], P('req', None, None, None, 'head'), may hold values from -250 to 250
- cached_length: int32 [64], P('req'), may hold values from 33 to 4096, as said below
- page_keeper: int32 [64, 128], P('req'), may hold values from -1 to 63, as said below
- page_slot_index: int32 [64, 128], P('req'), may hold values from -1 to 1, as said below
- memory_state: float32 [2, 64, 8, 128, 128], P(None, 'req', 'head'), may hold values from -3 to 3
- retention: float32 [64, 8], P('req', 'head'), may hold values from 0.2 to 1
- momentum: float32 [64, 8], P('req', 'head'), may hold values from 0.2 to 0.9
- memory_step_scale: float32 [64, 8], P('req', 'head'), may hold values from 0.02 to 0.3
- halving_updates: int32 [64, 8], P('req'), may hold values 0 or 1
Outputs:
- layer_out: bfloat16 [64, 512, 1024], P('req', 'head')
- new_state: float32 [2, 64, 8, 128, 128], P(None, 'req', 'head')
Inputs may be any that keep to these rules, and one draw needn't show every extreme that they name: `cached_length`: the requests of one device hold together at most 128 pages. `page_keeper`: pages j below cached_length[r] / 32 (rounded up) have a keeper; later entries are -1. No keeper and slot serve two pages of the requests of one device. `page_slot_index`: -1 exactly where page_keeper is -1.
All inputs are finite; a program needn't handle non-finite values. No bound on the sum of `halving_updates` on one device may be relied on, other than what follows from the above.
Results may differ from a plain program's by a relative error of at most 0.012.
The roundings to bfloat16 on the way count: a program that leaves them out, or rounds other values in their place, can miss the bound.
Values may be sent and summed in bfloat16 or wider, within the bound.
A program may use at most 64 MiB of HBM per device.

v0:
```python
import math
import jax
import jax.numpy as jnp
from jax import lax
from jax.sharding import PartitionSpec as P

HD = 128
BLK = 64
PAGE = 32
norm_eps = 1e-05
unit_eps = 1e-06


def unit_rows(values_f):
    return values_f * lax.rsqrt(jnp.sum(values_f * values_f, axis=-1, keepdims=True) + unit_eps)


def against(left, right):
    return lax.dot_general(
        left, right, (((1,), (1,)), ((), ())), preferred_element_type=jnp.float32
    )


def exact_rows(left, right):
    return lax.dot_general(
        left,
        right,
        (((1,), (1,)), ((), ())),
        precision=lax.Precision.HIGHEST,
        preferred_element_type=jnp.float32,
    )


def exact_outer(left, right):
    return lax.dot_general(
        left,
        right,
        (((0,), (0,)), ((), ())),
        precision=lax.Precision.HIGHEST,
        preferred_element_type=jnp.float32,
    )


def shards(
    tokens,
    gain,
    projection_weight,
    output_weight,
    persist,
    cache_page_slots,
    cached_length,
    page_keeper,
    page_slot_index,
    memory_state,
    retention,
    momentum,
    memory_step_scale,
    halving_updates,
):
    req_dev = tokens.shape[0]
    width = tokens.shape[2]
    head_cols = projection_weight.shape[2]
    homes = cache_page_slots.shape[1]
    lanes = cache_page_slots.shape[2] // PAGE
    max_pages = page_keeper.shape[1]
    scale = 1.0 / math.sqrt(HD)
    gain_f = gain.astype(jnp.float32)
    flat_w = projection_weight.reshape(width, 4 * head_cols)
    piece_f = lax.all_gather(tokens, "head", axis=1, tiled=True).astype(jnp.float32)
    scaled = (
        piece_f * lax.rsqrt(jnp.mean(piece_f * piece_f, axis=-1, keepdims=True) + norm_eps) * gain_f
    )
    normed = scaled.astype(jnp.bfloat16)
    count = normed.shape[0] * normed.shape[1]
    result = jnp.dot(normed.reshape(count, width), flat_w, preferred_element_type=jnp.float32)
    projected = result.reshape(normed.shape[0], normed.shape[1], 4, head_cols)
    queries = projected[:, :, 0].astype(jnp.bfloat16)
    own_keys = projected[:, :, 1].astype(jnp.bfloat16)
    own_values = projected[:, :, 2].astype(jnp.bfloat16)
    gates = projected[:, :, 3]
    prefill = queries.shape[1]
    kept_span = lanes * PAGE
    received = lax.all_to_all(cache_page_slots, "req", split_axis=1, concat_axis=0, tiled=True)
    cache_keys = received[:, 0, :, 0, :].reshape(homes * kept_span, head_cols)
    cache_values = received[:, 0, :, 1, :].reshape(homes * kept_span, head_cols)
    page_ids = jnp.arange(max_pages, dtype=jnp.int32)
    filled = jnp.clip(cached_length[:, None] - page_ids[None, :] * PAGE, 0, PAGE)
    slot_of = page_keeper * lanes + page_slot_index
    slot_ids = jnp.arange(homes * lanes, dtype=jnp.int32)
    slot_fill = jnp.sum(
        jnp.where(slot_of[:, :, None] == slot_ids[None, None, :], filled[:, :, None], 0), axis=1
    )
    position = jnp.arange(PAGE, dtype=jnp.int32)
    full_valid = (position[None, None, :] < slot_fill[:, :, None]).reshape(
        req_dev, homes, lanes * PAGE
    )
    cache_valid = full_valid.reshape(req_dev, homes * kept_span)
    causal = jnp.arange(prefill)[:, None] >= jnp.arange(prefill)[None, :]
    upper_col = HD
    query_head = queries[0, :, 0:upper_col]
    key_head = own_keys[0, :, 0:upper_col]
    value_head = own_values[0, :, 0:upper_col]
    score_p = against(query_head, persist[0, :, 0:upper_col]) * scale
    score_c = jnp.where(cache_valid[0][None, :], against(query_head, cache_keys) * scale, -jnp.inf)
    score_t = jnp.where(causal, against(query_head, key_head) * scale, -jnp.inf)
    row_max = jnp.maximum(
        jnp.maximum(
            jnp.max(score_p, axis=-1, keepdims=True), jnp.max(score_c, axis=-1, keepdims=True)
        ),
        jnp.max(score_t, axis=-1, keepdims=True),
    )
    exp_p = jnp.exp(score_p - row_max)
    exp_c = jnp.exp(score_c - row_max)
    exp_t = jnp.exp(score_t - row_max)
    total = (
        jnp.sum(exp_p, axis=-1, keepdims=True)
        + jnp.sum(exp_c, axis=-1, keepdims=True)
        + jnp.sum(exp_t, axis=-1, keepdims=True)
    )
    mixed = jnp.dot(
        exp_p.astype(jnp.bfloat16), persist[1, :, 0:upper_col], preferred_element_type=jnp.float32
    )
    mixed = mixed + jnp.dot(
        exp_c.astype(jnp.bfloat16), cache_values, preferred_element_type=jnp.float32
    )
    mixed = mixed + jnp.dot(
        exp_t.astype(jnp.bfloat16), value_head, preferred_element_type=jnp.float32
    )
    attended = mixed / total
    unit_attn = attended * lax.rsqrt(
        jnp.mean(attended * attended, axis=-1, keepdims=True) + unit_eps
    )
    query_unit = unit_rows(query_head.astype(jnp.float32))
    key_unit = unit_rows(key_head.astype(jnp.float32))
    value_f = value_head.astype(jnp.float32)
    state_m = memory_state[0, 0, 0]
    state_s = memory_state[1, 0, 0]
    reads = []
    for block_span in range(prefill // BLK):
        lower = block_span * BLK
        q_block = query_unit[lower : lower + BLK]
        k_block = key_unit[lower : lower + BLK]
        v_block = value_f[lower : lower + BLK]
        reads.append(exact_rows(q_block, state_m))
        errors = exact_rows(k_block, state_m) - v_block
        grads = exact_outer(errors, k_block)
        state_s = momentum[0, 0] * state_s - memory_step_scale[0, 0] * grads
        keeper_list = retention[0, 0] * jnp.where(halving_updates[0, block_span] == 1, 0.5, 1.0)
        state_m = keeper_list * state_m + state_s
    memory_read = jnp.concatenate(reads, axis=0)
    head_outs = unit_attn + jax.nn.sigmoid(gates[0, :, 0:upper_col]) * memory_read
    head_states = [jnp.stack([state_m, state_s])]
    request_outs = [head_outs.astype(jnp.bfloat16)]
    state_rows = [jnp.stack(head_states, axis=1)]
    mixed_heads = jnp.stack(request_outs)
    new_state = jnp.stack(state_rows, axis=1)
    regrouped = lax.all_to_all(mixed_heads, "head", split_axis=1, concat_axis=2, tiled=True)
    row_count = regrouped.shape[1]
    piece = lax.all_gather(output_weight, "head", axis=0, tiled=True)
    groups = piece.shape[0] // head_cols
    section = regrouped
    section = section.reshape(req_dev, row_count, groups, head_cols)
    blocks = piece.reshape(groups, head_cols, width)
    sums = jnp.einsum("atgc,gcd->atgd", section, blocks, preferred_element_type=jnp.float32)
    rounded = lax.optimization_barrier(sums.astype(jnp.bfloat16))
    layer_f = jnp.sum(rounded.astype(jnp.float32), axis=2)
    return (layer_f.astype(jnp.bfloat16), new_state)


def solution(mesh):
    in_specs = (
        P("req", "head", None),
        P(),
        P(None, None, "head"),
        P("head", None),
        P(None, None, "head"),
        P("req", None, None, None, "head"),
        P("req"),
        P("req", None),
        P("req", None),
        P(None, "req", "head", None, None),
        P("req", "head"),
        P("req", "head"),
        P("req", "head"),
        P("req", None),
    )
    out_specs = (P("req", "head", None), P(None, "req", "head", None, None))
    return jax.shard_map(shards, mesh=mesh, in_specs=in_specs, out_specs=out_specs, check_vma=False)
```

profile of v0, /device:TPU:1, one launch (start us, length us, event | category | flops | bytes accessed | tf_op | source)
XLA Modules:
  0.0 161.1 jit_solution(271079519594700890)
XLA Ops:
  7.3 0.7 all-gather.3.cloned.1.call-update
  7.9 3.5 %copy.44 = bf16[1,64,64,2,128]{4,2,3,0,1:T(8,128)(2,1)} copy(bf16[1,64,64,2,128]{4,3,2,1,0:T(2,128)(2,1)} %param.19) | data formatting | bytes 4194304 | tf_op args[5]
  11.4 19.2 %all-to-all-start = ((bf16[1,64,64,2,128]{4,2,3,0,1:T(8,128)(2,1)}), bf16[1,64,64,2,128]{4,2,3,0,1:T(8,128)(2,1)S(1)}, u32[]{:S(2)}, u32[]{:S(2)}) async-start(bf16[1,64,64,2,128]{4,2,3,0,1:T(8,128)(2,1)} %copy.44), calls=%async_computation | async-start | bytes 4194304 | tf_op jit(solution)/shard_map/all_to_all | solution.py:83
  30.7 0.7 all-gather.5.cloned.1.call-update
  31.4 1.4 copy.60
  32.9 1.3 copy.43
  34.2 0.7 fusion.85
  43.0 3.8 %all-gather.3.cloned.1.call-done = bf16[1,512,1024]{2,1,0:T(8,128)(2,1)} async-done(((bf16[1,64,1024]{2,1,0:T(8,128)(2,1)}), bf16[1,512,1024]{2,1,0:T(8,128)(2,1)}) %all-gather.3.cloned.1.call-update) | async-done | bytes 1048592 | tf_op jit(solution)/shard_map/all_gather | solution.py:69
  46.8 1.5 fusion.6
  48.3 2.3 %convolution_bitcast_fusion = f32[1,512,4,128]{3,1,2,0:T(8,128)S(1)} fusion(bf16[4,128,1024]{2,1,0:T(8,128)(2,1)} %bitcast.161, bf16[1,512,1024]{2,1,0:T(8,128)(2,1)} %all-gather.3.cloned.1.call-done, f32[1024]{0:T(1024)S(1)} %convert_element_type.76, f32[512]{0:T(512)S(1)} %add_rsqrt_fusion.3), kind=kOutput, calls=%fused_computation.17 | convolution fusion | flops 538968064 | bytes 3151872 | tf_op jit(solution)/shard_map/dot_general | solution.py:75
  51.2 0.2 convolution_dynamic-update-slice_fusion.7
  51.5 0.2 convolution_subtract_fusion.7
  51.7 0.3 fusion.43
  52.0 0.2 convolution_dynamic-update-slice_fusion.6
  52.3 0.2 convolution_subtract_fusion.6
  52.5 0.3 multiply_add_fusion.5
  52.8 0.2 convolution_dynamic-update-slice_fusion.5
  53.1 0.2 convolution_subtract_fusion.5
  53.3 0.3 multiply_add_fusion.4
  53.6 0.2 convolution_dynamic-update-slice_fusion.4
  53.9 0.2 convolution_subtract_fusion.4
  54.1 0.3 multiply_add_fusion.3
  54.4 0.2 convolution_dynamic-update-slice_fusion.3
  54.7 0.2 convolution_subtract_fusion.3
  54.9 0.3 multiply_add_fusion.2
  55.2 0.2 convolution_dynamic-update-slice_fusion.2
  55.5 0.2 convolution_subtract_fusion.2
  55.7 0.3 multiply_add_fusion.1
  56.0 0.2 convolution_dynamic-update-slice_fusion.1
  56.3 0.2 convolution_subtract_fusion.1
  56.5 0.3 multiply_add_fusion
  56.8 0.2 convolution_dynamic-update-slice_fusion
  57.1 0.2 convolution_subtract_fusion
  57.5 0.3 fusion.12
  57.8 0.3 fusion.86
  58.1 67.5 %all-to-all-done = bf16[1,64,64,2,128]{4,2,3,0,1:T(8,128)(2,1)S(1)} async-done(((bf16[1,64,64,2,128]{4,2,3,0,1:T(8,128)(2,1)}), bf16[1,64,64,2,128]{4,2,3,0,1:T(8,128)(2,1)S(1)}, u32[]{:S(2)}, u32[]{:S(2)}) %all-to-all-start) | async-done | bytes 2097184 | tf_op jit(solution)/shard_map/all_to_all | solution.py:83
  126.0 1.4 fusion
  127.7 2.2 %fusion.1 = f32[512]{0:T(512)S(1)} fusion(f32[512,4096]{1,0:T(8,128)S(1)} %get-tuple-element.44, f32[512]{0:T(512)S(1)} %maximum_maximum_fusion, pred[4096]{0:T(1024)(128)(4,1)S(1)} %lt.27), kind=kLoop, calls=%fused_computation.3 | loop fusion | flops 8388096 | bytes 8396800 | tf_op jit(solution)/shard_map/reduce_sum | solution.py:117
  129.9 1.7 %fusion.3 = f32[512,128]{1,0:T(8,128)S(1)} fusion(bf16[4096,128]{1,0:T(8,128)(2,1)S(1)} %bitcast.162, f32[512,4096]{1,0:T(8,128)S(1)} %get-tuple-element.44, f32[512]{0:T(512)S(1)} %maximum_maximum_fusion, pred[4096]{0:T(1024)(128)(4,1)S(1)} %lt.27), kind=kOutput, calls=%fused_computation.5 | convolution fusion | flops 545259520 | bytes 9705472 | tf_op jit(solution)/shard_map/dot_general | solution.py:123
  131.9 0.5 multiply_reduce_fusion
  132.7 0.5 broadcast.141
  133.2 1.4 reduce.4
  134.7 0.7 reshape.270
  135.3 10.6 %all-to-all-start.1 = ((bf16[8,2,4096]{2,1,0:T(2,128)(2,1)}), bf16[8,2,4096]{2,1,0:T(2,128)(2,1)S(1)}, u32[]{:S(2)}, u32[]{:S(2)}) async-start(bf16[8,2,4096]{2,1,0:T(2,128)(2,1)} %reshape.270), calls=%async_computation.1 | async-start | bytes 262144 | tf_op jit(solution)/shard_map/all_to_all | solution.py:157
  146.0 0.7 maximum_bitcast_fusion
  146.6 4.6 %all-to-all-done.1 = bf16[8,2,4096]{2,1,0:T(2,128)(2,1)S(1)} async-done(((bf16[8,2,4096]{2,1,0:T(2,128)(2,1)}), bf16[8,2,4096]{2,1,0:T(2,128)(2,1)S(1)}, u32[]{:S(2)}, u32[]{:S(2)}) %all-to-all-start.1) | async-done | bytes 131104 | tf_op jit(solution)/shard_map/all_to_all | solution.py:157
  151.4 2.0 %fusion.9 = bf16[1,64,8,1024]{3,1,2,0:T(8,128)(2,1)S(1)} fusion(bf16[64,8,128]{2,0,1:T(8,128)(2,1)S(1)} %bitcast.164, bf16[8,128,1024]{2,1,0:T(8,128)(2,1)} %bitcast.157), kind=kOutput, calls=%fused_computation.14 | convolution fusion | flops 134742016 | bytes 3276800 | tf_op jit(solution)/shard_map/atgc,gcd->atgd/dot_general | solution.py:164
  153.4 0.8 reduce_sum.94
  (53 shorter events, 2.6 us)
Async XLA Ops:
  7.2 27.0 %copy-start.7 = (bf16[1024]{0:T(1024)(128)(2,1)S(1)}, bf16[1024]{0:T(1024)(128)(2,1)}, u32[]{:S(2)}) copy-start(bf16[1024]{0:T(1024)(128)(2,1)} %param.15) | copy-start | bytes 6148
  7.2 27.0 %copy-start.5 = (s32[1,8]{1,0:T(1,128)S(1)}, s32[1,8]{1,0:T(1,128)}, u32[]{:S(2)}) copy-start(s32[1,8]{1,0:T(1,128)} %param.27) | copy-start | bytes 100
  7.2 35.4 %copy-start.9 = (s32[1,128]{1,0:T(1,128)S(1)}, s32[1,128]{1,0:T(1,128)}, u32[]{:S(2)}) copy-start(s32[1,128]{1,0:T(1,128)} %param.21) | copy-start | bytes 1540
  7.2 35.4 %copy-start.8 = (s32[1,128]{1,0:T(1,128)S(1)}, s32[1,128]{1,0:T(1,128)}, u32[]{:S(2)}) copy-start(s32[1,128]{1,0:T(1,128)} %param.22) | copy-start | bytes 1540
  7.2 39.6 %all-gather.3.cloned.1.call-start = ((), (), s32[]{:S(2)}) async-start(), calls=%async_computation.2 | async-start | bytes 1179648 | tf_op jit(solution)/shard_map/all_gather | solution.py:69
  11.4 39.8 %copy-start.4 = (f32[2,1,1,128,128]{4,3,2,1,0:T(8,128)S(1)}, f32[2,1,1,128,128]{4,3,2,1,0:T(8,128)}, u32[]{:S(2)}) copy-start(f32[2,1,1,128,128]{4,3,2,1,0:T(8,128)} %param.23) | copy-start | bytes 393220
  11.4 114.3 %all-to-all-start = ((bf16[1,64,64,2,128]{4,2,3,0,1:T(8,128)(2,1)}), bf16[1,64,64,2,128]{4,2,3,0,1:T(8,128)(2,1)S(1)}, u32[]{:S(2)}, u32[]{:S(2)}) async-start(bf16[1,64,64,2,128]{4,2,3,0,1:T(8,128)(2,1)} %copy.44), calls=%async_computation | async-start | bytes 4194304 | tf_op jit(solution)/shard_map/all_to_all | solution.py:83
  30.7 26.6 %copy-start.6 = (bf16[2,16,128]{2,1,0:T(8,128)(2,1)S(1)}, bf16[2,16,128]{2,1,0:T(8,128)(2,1)}, u32[]{:S(2)}) copy-start(bf16[2,16,128]{2,1,0:T(8,128)(2,1)} %param.18) | copy-start | bytes 24580
  30.7 120.7 %all-gather.5.cloned.1.call-start = ((), (), s32[]{:S(2)}) async-start(), calls=%async_computation.3 | async-start | bytes 2359296 | tf_op jit(solution)/shard_map/all_gather | solution.py:159
  50.6 7.2 %copy-start = (f32[1,512,4,128]{3,1,2,0:T(8,128)}, f32[1,512,4,128]{3,1,2,0:T(8,128)S(1)}, u32[]{:S(2)}) copy-start(f32[1,512,4,128]{3,1,2,0:T(8,128)S(1)} %convolution_bitcast_fusion) | copy-start | bytes 3145732
  57.0 0.7 copy-start.2
  129.9 2.0 %copy-start.1 = (f32[1,512,4,128]{3,1,2,0:T(8,128)S(1)}, f32[1,512,4,128]{3,1,2,0:T(8,128)}, u32[]{:S(2)}) copy-start(f32[1,512,4,128]{3,1,2,0:T(8,128)} %copy-done) | copy-start | bytes 3145732
  129.9 2.5 %copy-start.3 = (f32[512,128]{1,0:T(8,128)S(1)}, f32[512,128]{1,0:T(8,128)}, u32[]{:S(2)}) copy-start(f32[512,128]{1,0:T(8,128)} %copy-done.2) | copy-start | bytes 786436
  135.3 15.9 %all-to-all-start.1 = ((bf16[8,2,4096]{2,1,0:T(2,128)(2,1)}), bf16[8,2,4096]{2,1,0:T(2,128)(2,1)S(1)}, u32[]{:S(2)}, u32[]{:S(2)}) async-start(bf16[8,2,4096]{2,1,0:T(2,128)(2,1)} %reshape.270), calls=%async_computation.1 | async-start | bytes 262144 | tf_op jit(solution)/shard_map/all_to_all | solution.py:157
Sparse Core Ops, SparseCore 0:
  10.2 36.6 all-gather.2
  49.0 32.9 all-gather.4
where the time goes:
time: 162 us; the launch traced here: 161 us
  waiting for transfers between devices  77.3 us (48%)
  starting transfers between devices  29.9 us (18%)
  between operations  22.2 us (14%)
  matrix products  14.8 us (9%)
  local copies, waits for them, and re-layouts  9.12 us (6%)
  other arithmetic  7.67 us (5%)
    all_to_all x1, waiting for transfers between devices, shards(): lax.all_to_all(cache_page_slots, 'req', split_axis=1, concat_axis=0, tile...  67.5 us
    all_to_all x1, starting transfers between devices, shards(): lax.all_to_all(cache_page_slots, 'req', split_axis=1, concat_axis=0, tile...  19.2 us
    all_to_all x1, starting transfers between devices, shards(): lax.all_to_all(mixed_heads, 'head', split_axis=1, concat_axis=2, tiled=True)  10.6 us
    unnamed x26, local copies, waits for them, and re-layouts  6.3 us
    all_to_all x1, waiting for transfers between devices, shards(): lax.all_to_all(mixed_heads, 'head', split_axis=1, concat_axis=2, tiled=True)  4.58 us
    dot_general x16, matrix products, exact_rows(): lax.dot_general(left, right, (((1,), (1,)), ((), ())), precision=lax.Prec...  3.83 us
    all_gather x1, waiting for transfers between devices, shards(): lax.all_gather(tokens, 'head', axis=1, tiled=True).astype(jnp.float32)  3.79 us
  transfers between devices with their start and end apart: 4, of which 3 were waited for; matrix products, arithmetic and copies ran while one was open for 18% of the time, Pallas kernels for 0%

commit v1 on v0

--- a/solution.py
+++ b/solution.py
@@ -66,7 +66,16 @@
     scale = 1.0 / math.sqrt(HD)
     gain_f = gain.astype(jnp.float32)
     flat_w = projection_weight.reshape(width, 4 * head_cols)
-    piece_f = lax.all_gather(tokens, "head", axis=1, tiled=True).astype(jnp.float32)
+    cycles_meet = lambda row_data, which_dim: jnp.concatenate(
+        lax.all_to_all(
+            jnp.stack(lax.axis_size("head") * [row_data], axis=0),
+            axis_name="head",
+            split_axis=0,
+            concat_axis=0,
+        ),
+        axis=which_dim,
+    )
+    piece_f = cycles_meet(tokens, 1).astype(jnp.float32)
     scaled = (
         piece_f * lax.rsqrt(jnp.mean(piece_f * piece_f, axis=-1, keepdims=True) + norm_eps) * gain_f
     )

time: 162 us -> 183 us (1.13)
  waiting for transfers between devices: 77.3 us -> 92 us
  starting transfers between devices: 29.9 us -> 33 us
  local copies, waits for them, and re-layouts: 9.12 us -> 12.1 us
    all_to_all x1, waiting for transfers between devices: 67.5 us -> 86.7 us  [shards(): lax.all_to_all(cache_page_slots, 'req', split_axis=1, concat_axis=0, tile...]
    all_to_all x0 -> x1, starting transfers between devices: none -> 10.3 us  [shards(): lax.all_to_all(jnp.stack(lax.axis_size('head') * [row_data], axis=0), axi...]
    all_to_all x1, starting transfers between devices: 19.2 us -> 14.1 us  [shards(): lax.all_to_all(cache_page_slots, 'req', split_axis=1, concat_axis=0, tile...]
    all_gather x1 -> x0, waiting for transfers between devices: 3.79 us -> none  [shards(): lax.all_gather(tokens, 'head', axis=1, tiled=True).astype(jnp.float32)]
    all_to_all x1, starting transfers between devices: 10.6 us -> 8.61 us  [shards(): lax.all_to_all(mixed_heads, 'head', split_axis=1, concat_axis=2, tiled=True)]
    another operation x0 -> x1, local copies, waits for them, and re-layouts: none -> 2.01 us  [shards(): jnp.stack(lax.axis_size('head') * [row_data], axis=0)]
    unnamed x26 -> x18, local copies, waits for them, and re-layouts: 6.3 us -> 6.29 us
  transfers between devices with their start and end apart: 4 -> 4, of which waited for: 3 -> 2; matrix products, arithmetic and copies ran while one was open for 18% -> 16% of each run, Pallas kernels for 0% -> 0%
where the time goes in v1:
time: 183 us; the launch traced here: 182 us
  waiting for transfers between devices  92 us (50%)
  starting transfers between devices  33 us (18%)
  between operations  22.2 us (12%)
  matrix products  14.5 us (8%)
  local copies, waits for them, and re-layouts  12.1 us (7%)
  other arithmetic  8.12 us (4%)
    all_to_all x1, waiting for transfers between devices, shards(): lax.all_to_all(cache_page_slots, 'req', split_axis=1, concat_axis=0, tile...  86.7 us
    all_to_all x1, starting transfers between devices, shards(): lax.all_to_all(cache_page_slots, 'req', split_axis=1, concat_axis=0, tile...  14.1 us
    all_to_all x1, starting transfers between devices, shards(): lax.all_to_all(jnp.stack(lax.axis_size('head') * [row_data], axis=0), axi...  10.3 us
    all_to_all x1, starting transfers between devices, shards(): lax.all_to_all(mixed_heads, 'head', split_axis=1, concat_axis=2, tiled=True)  8.61 us
    unnamed x18, local copies, waits for them, and re-layouts  6.29 us
    all_to_all x1, waiting for transfers between devices, shards(): lax.all_to_all(mixed_heads, 'head', split_axis=1, concat_axis=2, tiled=True)  4.58 us
    dot_general x16, matrix products, exact_rows(): lax.dot_general(left, right, (((1,), (1,)), ((), ())), precision=lax.Prec...  3.83 us
  transfers between devices with their start and end apart: 4, of which 2 were waited for; matrix products, arithmetic and copies ran while one was open for 16% of the time, Pallas kernels for 0%

profile of v1, /device:TPU:1, one launch (start us, length us, event | category | flops | bytes accessed | tf_op | source)
XLA Modules:
  0.0 181.9 jit_solution(17519912648984389074)
XLA Ops:
  7.2 2.0 %stack.10 = bf16[8,1,64,1024]{3,2,1,0:T(8,128)(2,1)} broadcast(bf16[64,1024]{1,0:T(8,128)(2,1)} %bitcast.167), dimensions={2,3} | broadcast | bytes 1179648 | tf_op jit(solution)/shard_map/stack | solution.py:71
  9.2 10.3 %all-to-all-start = ((bf16[8,1,64,1024]{3,2,1,0:T(8,128)(2,1)}), bf16[8,1,64,1024]{3,2,1,0:T(8,128)(2,1)S(1)}, u32[]{:S(2)}, u32[]{:S(2)}) async-start(bf16[8,1,64,1024]{3,2,1,0:T(8,128)(2,1)} %stack.10), calls=%async_computation | async-start | bytes 2097152 | tf_op jit(solution)/shard_map/all_to_all | solution.py:70
  19.5 0.7 all-gather.2.cloned.1.call-update
  20.2 0.7 convert_element_type.92
  20.9 1.4 copy.60
  22.3 1.3 copy.43
  25.6 1.6 fusion.81
  33.0 0.7 add_bitcast_fusion.1
  34.0 3.5 %copy.44 = bf16[1,64,64,2,128]{4,2,3,0,1:T(8,128)(2,1)} copy(bf16[1,64,64,2,128]{4,3,2,1,0:T(2,128)(2,1)} %param.19) | data formatting | bytes 4194304 | tf_op args[5]
  37.6 14.1 %all-to-all-start.1 = ((bf16[1,64,64,2,128]{4,2,3,0,1:T(8,128)(2,1)}), bf16[1,64,64,2,128]{4,2,3,0,1:T(8,128)(2,1)S(1)}, u32[]{:S(2)}, u32[]{:S(2)}) async-start(bf16[1,64,64,2,128]{4,2,3,0,1:T(8,128)(2,1)} %copy.44), calls=%async_computation.1 | async-start | bytes 4194304 | tf_op jit(solution)/shard_map/all_to_all | solution.py:92
  51.7 0.3 fusion.6
  52.0 0.3 fusion.8
  52.3 2.0 %convolution_bitcast_fusion = f32[1,512,4,128]{3,1,2,0:T(8,128)S(1)} fusion(bf16[512,1024,1]{1,0,2:T(8,128)(2,1)S(1)} %bitcast.163, bf16[4,128,1024]{2,1,0:T(8,128)(2,1)} %bitcast.162), kind=kOutput, calls=%fused_computation.17 | convolution fusion | flops 536870912 | bytes 3145728 | tf_op jit(solution)/shard_map/dot_general | solution.py:84
  54.8 0.2 convolution_dynamic-update-slice_fusion.7
  55.1 0.2 convolution_subtract_fusion.7
  55.4 0.3 fusion.39
  55.7 0.2 convolution_dynamic-update-slice_fusion.6
  55.9 0.2 convolution_subtract_fusion.6
  56.2 0.3 multiply_add_fusion.5
  56.5 0.2 convolution_dynamic-update-slice_fusion.5
  56.7 0.2 convolution_subtract_fusion.5
  57.0 0.3 multiply_add_fusion.4
  57.5 0.2 convolution_subtract_fusion.4
  57.8 0.3 multiply_add_fusion.3
  58.3 0.2 convolution_subtract_fusion.3
  58.5 0.3 multiply_add_fusion.2
  58.8 0.2 convolution_dynamic-update-slice_fusion.2
  59.1 0.2 convolution_subtract_fusion.2
  59.3 0.3 multiply_add_fusion.1
  59.6 0.2 convolution_dynamic-update-slice_fusion.1
  59.9 0.2 convolution_subtract_fusion.1
  60.1 0.3 multiply_add_fusion
  60.7 0.2 convolution_subtract_fusion
  61.1 0.3 fusion.12
  61.5 0.3 fusion.82
  61.8 86.7 %all-to-all-done.1 = bf16[1,64,64,2,128]{4,2,3,0,1:T(8,128)(2,1)S(1)} async-done(((bf16[1,64,64,2,128]{4,2,3,0,1:T(8,128)(2,1)}), bf16[1,64,64,2,128]{4,2,3,0,1:T(8,128)(2,1)S(1)}, u32[]{:S(2)}, u32[]{:S(2)}) %all-to-all-start.1) | async-done | bytes 2097184 | tf_op jit(solution)/shard_map/all_to_all | solution.py:92
  148.9 1.4 fusion
  150.5 2.2 %fusion.1 = f32[512]{0:T(512)S(1)} fusion(f32[512,4096]{1,0:T(8,128)S(1)} %get-tuple-element.44, f32[512]{0:T(512)S(1)} %maximum_maximum_fusion, pred[4096]{0:T(1024)(128)(4,1)S(1)} %lt.27), kind=kLoop, calls=%fused_computation.3 | loop fusion | flops 8388096 | bytes 8396800 | tf_op jit(solution)/shard_map/reduce_sum | solution.py:126
  152.7 1.7 fusion.3
  154.7 0.5 multiply_reduce_fusion
  155.6 0.5 broadcast.164
  156.1 1.4 reduce.5
  157.5 0.7 reshape.316
  158.2 8.6 %all-to-all-start.2 = ((bf16[8,2,4096]{2,1,0:T(2,128)(2,1)}), bf16[8,2,4096]{2,1,0:T(2,128)(2,1)S(1)}, u32[]{:S(2)}, u32[]{:S(2)}) async-start(bf16[8,2,4096]{2,1,0:T(2,128)(2,1)} %reshape.316), calls=%async_computation.2 | async-start | bytes 262144 | tf_op jit(solution)/shard_map/all_to_all | solution.py:166
  166.8 0.7 maximum_bitcast_fusion
  167.4 4.6 %all-to-all-done.2 = bf16[8,2,4096]{2,1,0:T(2,128)(2,1)S(1)} async-done(((bf16[8,2,4096]{2,1,0:T(2,128)(2,1)}), bf16[8,2,4096]{2,1,0:T(2,128)(2,1)S(1)}, u32[]{:S(2)}, u32[]{:S(2)}) %all-to-all-start.2) | async-done | bytes 131104 | tf_op jit(solution)/shard_map/all_to_all | solution.py:166
  172.2 2.0 %fusion.9 = bf16[1,64,8,1024]{3,1,2,0:T(8,128)(2,1)S(1)} fusion(bf16[64,8,128]{2,0,1:T(8,128)(2,1)S(1)} %bitcast.166, bf16[8,128,1024]{2,1,0:T(8,128)(2,1)} %bitcast.158), kind=kOutput, calls=%fused_computation.14 | convolution fusion | flops 134742016 | bytes 3276800 | tf_op jit(solution)/shard_map/atgc,gcd->atgd/dot_general | solution.py:173
  174.2 0.8 reduce_sum.94
  (46 shorter events, 3.2 us)
Async XLA Ops:
  9.2 28.4 %all-to-all-start = ((bf16[8,1,64,1024]{3,2,1,0:T(8,128)(2,1)}), bf16[8,1,64,1024]{3,2,1,0:T(8,128)(2,1)S(1)}, u32[]{:S(2)}, u32[]{:S(2)}) async-start(bf16[8,1,64,1024]{3,2,1,0:T(8,128)(2,1)} %stack.10), calls=%async_computation | async-start | bytes 2097152 | tf_op jit(solution)/shard_map/all_to_all | solution.py:70
  19.5 152.7 %all-gather.2.cloned.1.call-start = ((), (), s32[]{:S(2)}) async-start(), calls=%async_computation.3 | async-start | bytes 2359296 | tf_op jit(solution)/shard_map/all_gather | solution.py:168
  34.0 20.8 %copy-start.4 = (f32[2,1,1,128,128]{4,3,2,1,0:T(8,128)S(1)}, f32[2,1,1,128,128]{4,3,2,1,0:T(8,128)}, u32[]{:S(2)}) copy-start(f32[2,1,1,128,128]{4,3,2,1,0:T(8,128)} %param.23) | copy-start | bytes 393220
  37.5 23.4 %copy-start.5 = (bf16[2,16,128]{2,1,0:T(8,128)(2,1)S(1)}, bf16[2,16,128]{2,1,0:T(8,128)(2,1)}, u32[]{:S(2)}) copy-start(bf16[2,16,128]{2,1,0:T(8,128)(2,1)} %param.18) | copy-start | bytes 24580
  37.6 111.0 %all-to-all-start.1 = ((bf16[1,64,64,2,128]{4,2,3,0,1:T(8,128)(2,1)}), bf16[1,64,64,2,128]{4,2,3,0,1:T(8,128)(2,1)S(1)}, u32[]{:S(2)}, u32[]{:S(2)}) async-start(bf16[1,64,64,2,128]{4,2,3,0,1:T(8,128)(2,1)} %copy.44), calls=%async_computation.1 | async-start | bytes 4194304 | tf_op jit(solution)/shard_map/all_to_all | solution.py:92
  54.3 7.2 %copy-start = (f32[1,512,4,128]{3,1,2,0:T(8,128)}, f32[1,512,4,128]{3,1,2,0:T(8,128)S(1)}, u32[]{:S(2)}) copy-start(f32[1,512,4,128]{3,1,2,0:T(8,128)S(1)} %convolution_bitcast_fusion) | copy-start | bytes 3145732
  60.7 0.7 copy-start.2
  152.7 2.0 %copy-start.1 = (f32[1,512,4,128]{3,1,2,0:T(8,128)S(1)}, f32[1,512,4,128]{3,1,2,0:T(8,128)}, u32[]{:S(2)}) copy-start(f32[1,512,4,128]{3,1,2,0:T(8,128)} %copy-done) | copy-start | bytes 3145732
  152.7 2.5 %copy-start.3 = (f32[512,128]{1,0:T(8,128)S(1)}, f32[512,128]{1,0:T(8,128)}, u32[]{:S(2)}) copy-start(f32[512,128]{1,0:T(8,128)} %copy-done.2) | copy-start | bytes 786436
  158.2 13.9 %all-to-all-start.2 = ((bf16[8,2,4096]{2,1,0:T(2,128)(2,1)}), bf16[8,2,4096]{2,1,0:T(2,128)(2,1)S(1)}, u32[]{:S(2)}, u32[]{:S(2)}) async-start(bf16[8,2,4096]{2,1,0:T(2,128)(2,1)} %reshape.316), calls=%async_computation.2 | async-start | bytes 262144 | tf_op jit(solution)/shard_map/all_to_all | solution.py:166
Sparse Core Ops, SparseCore 0:
  22.4 33.2 all-gather.1
